TPU v7x, 32 devices: a whole 2x2x4 slice. The times are simulated.
32 devices in a mesh: dp: 8 (over z, x), mp: 4 (over y, core).
Axes of the slice: x: 2, y: 2, z: 4, core: 2. Of those that a mesh axis runs over, the one named last changes fastest.
Arguments:
- mel_frames: float32 [16384, 80], P('dp')
- frame_mask: int32 [8, 1024], replicated, may hold values from 0 to 1, as said below
- token_ids: int32 [8, 384], replicated, may hold values from 0 to 51839
- token_mask: int32 [8, 384], replicated, may hold values from 0 to 1, as said below
- embedding: float32 [51840, 768], P('dp', 'mp'), may hold values from -6 to 6
- conv_one: float32 [3, 80, 768], P(None, None, ('dp', 'mp')), may hold values from -0.375 to 0.375
- conv_two: float32 [3, 768, 768], P(None, ('dp', 'mp')), may hold values from -0.125 to 0.125
- enc_qkv: float32 [3, 768, 768], P(None, 'dp', 'mp'), may hold values from -0.21875 to 0.21875
- enc_out: float32 [768, 768], P('mp', 'dp'), may hold values from -3.5 to 3.5
- enc_up: float32 [768, 3072], P('dp', 'mp'), may hold values from -0.21875 to 0.21875
- enc_down: float32 [3072, 768], P('mp', 'dp'), may hold values from -0.109375 to 0.109375
- cross_qkv: float32 [3, 768, 768], P(None, 'dp', 'mp'), may hold values from -0.21875 to 0.21875
- cross_out: float32 [768, 768], P('mp', 'dp'), may hold values from -3.5 to 3.5
- dec_qkv: float32 [3, 768, 768], P(None, 'dp', 'mp'), may hold values from -0.21875 to 0.21875
- dec_out: float32 [768, 768], P('mp', 'dp'), may hold values from -1.75 to 1.75
- dec_up: float32 [768, 3072], P('dp', 'mp'), may hold values from -0.21875 to 0.21875
- dec_down: float32 [3072, 768], P('mp', 'dp'), may hold values from -0.109375 to 0.109375
- norm_params: float32 [6, 2, 768], P(None, None, 'dp'), as said below
- cotangent: float32 [3072, 768], P('dp'), may hold values from -6 to 6
Outputs:
- decoded: float32 [3072, 768], P('dp')
- mel_grad: float32 [16384, 80], P('dp')
- embed_grad: float32 [51840, 768], P('dp', 'mp')
- conv_one_grad: float32 [3, 80, 768], P(None, None, ('dp', 'mp'))
- conv_two_grad: float32 [3, 768, 768], P(None, ('dp', 'mp'))
- enc_qkv_grad: float32 [3, 768, 768], P(None, 'dp', 'mp')
- enc_out_grad: float32 [768, 768], P('mp', 'dp')
- enc_up_grad: float32 [768, 3072], P('dp', 'mp')
- enc_down_grad: float32 [3072, 768], P('mp', 'dp')
- cross_qkv_grad: float32 [3, 768, 768], P(None, 'dp', 'mp')
- cross_out_grad: float32 [768, 768], P('mp', 'dp')
- dec_qkv_grad: float32 [3, 768, 768], P(None, 'dp', 'mp')
- dec_out_grad: float32 [768, 768], P('mp', 'dp')
- dec_up_grad: float32 [768, 3072], P('dp', 'mp')
- dec_down_grad: float32 [3072, 768], P('mp', 'dp')
- norm_grad: float32 [6, 2, 768], P(None, None, 'dp')
- rms_stats: float32 [9], replicated
Inputs may be any that keep to these rules, and one draw needn't show every extreme that they name: `frame_mask`: each clip's row is 1 on a prefix of at least max(68, 1) frames and 0 after it; some clip is valid in full. `token_mask`: each clip's row is 1 on a prefix of at least max(24, 1) tokens and 0 after it; some clip is valid in full. `norm_params`: gains near one and biases near zero.
All inputs are finite; a program needn't handle non-finite values.
Results may differ from a plain program's by a relative error of at most 0.0003.
Values sent between devices are 32-bit elements; how exact they have to be, the bound alone decides.
A program may use at most 256 MiB of HBM per device.

v0:
```python
import math
import jax
import jax.numpy as jnp
from jax import lax
from jax.sharding import PartitionSpec as P

HEAD = 64
HIGH = lax.Precision.HIGHEST
NEG = -1e30
EPS = 1e-05


def matmul(left, right):
    return jnp.dot(left, right, precision=HIGH, preferred_element_type=jnp.float32)


def gelu_exact(tensor):
    return jax.nn.gelu(tensor, approximate=False)


def layer_norm(tensor, norm_param):
    centre = tensor - jnp.mean(tensor, axis=-1, keepdims=True)
    spread = jnp.mean(centre * centre, axis=-1, keepdims=True)
    return centre * lax.rsqrt(spread + EPS) * norm_param[0] + norm_param[1]


def sinusoid(position, model_width):
    half_width = model_width // 2
    inverse_rates = jnp.exp(
        -math.log(10000.0) * jnp.arange(half_width).astype(jnp.float32) / (half_width - 1)
    )
    angles = position.astype(jnp.float32)[:, None] * inverse_rates[None, :]
    return jnp.concatenate([jnp.sin(angles), jnp.cos(angles)], axis=1)


def split_heads(tensor):
    return tensor.reshape(tensor.shape[0], -1, HEAD)


def attend(queries, key_rows, values, allowed):
    factor = 1.0 / math.sqrt(queries.shape[-1])
    scores = jnp.einsum("qhe,khe->hqk", queries, key_rows, precision=HIGH) * factor
    scores = jnp.where(allowed[None], scores, NEG)
    peaks = jnp.max(scores, axis=-1, keepdims=True)
    weight = jnp.exp(scores - peaks)
    totals = jnp.sum(weight, axis=-1, keepdims=True)
    output = jnp.einsum("hqk,khe->qhe", weight / totals, values, precision=HIGH)
    return (output, peaks + jnp.log(totals))


def attention_grads(queries, key_rows, values, allowed, output, log_total, grad_flat):
    factor = 1.0 / math.sqrt(queries.shape[-1])
    grad_out = grad_flat.reshape(output.shape)
    scores = jnp.einsum("qhe,khe->hqk", queries, key_rows, precision=HIGH) * factor
    attn_probs = jnp.where(allowed[None], jnp.exp(scores - log_total), 0.0)
    grad_values = jnp.einsum("hqk,qhe->khe", attn_probs, grad_out, precision=HIGH)
    grad_probs = jnp.einsum("qhe,khe->hqk", grad_out, values, precision=HIGH)
    inner_dot = jnp.sum(grad_out * output, axis=-1)
    grad_scores = attn_probs * (grad_probs - inner_dot.T[:, :, None]) * factor
    grad_queries = jnp.einsum("hqk,khe->qhe", grad_scores, key_rows, precision=HIGH)
    grad_keys = jnp.einsum("hqk,qhe->khe", grad_scores, queries, precision=HIGH)
    return (
        grad_queries.reshape(grad_queries.shape[0], -1),
        grad_keys.reshape(grad_keys.shape[0], -1),
        grad_values.reshape(grad_values.shape[0], -1),
    )


def project_three(rows_in, norm_param, weight):
    normed = layer_norm(rows_in, norm_param)
    return (matmul(normed, weight[0]), matmul(normed, weight[1]), matmul(normed, weight[2]))


def project_pair(rows_in, norm_param, weight_keys, weight_values):
    normed = layer_norm(rows_in, norm_param)
    return (matmul(normed, weight_keys), matmul(normed, weight_values))


def project_one(rows_in, norm_param, weight):
    return matmul(layer_norm(rows_in, norm_param), weight)


def feed_forward(rows_in, norm_param, up_weight, down_weight):
    return matmul(gelu_exact(matmul(layer_norm(rows_in, norm_param), up_weight)), down_weight)


def stem_piece(mel_in, weight_one, weight_two):
    mel_rows = mel_in.shape[0]
    padded = jnp.pad(mel_in, ((1, 1), (0, 0)))
    activated = gelu_exact(
        matmul(padded[0:mel_rows], weight_one[0])
        + matmul(padded[1 : mel_rows + 1], weight_one[1])
        + matmul(padded[2 : mel_rows + 2], weight_one[2])
    )
    padded_one = jnp.pad(activated, ((1, 1), (0, 0)))
    return (
        matmul(padded_one[0:mel_rows:2], weight_two[0])
        + matmul(padded_one[1 : mel_rows + 1 : 2], weight_two[1])
        + matmul(padded_one[2 : mel_rows + 2 : 2], weight_two[2])
    )


def masked_squares(tensor, row_weight):
    return jnp.sum(row_weight[:, None] * tensor * tensor)


def branch_sum(tensor):
    return lax.psum(tensor, "mp")


def input_sum(grad_rows, grad_norm):
    return lax.psum((grad_rows, grad_norm), "mp")


def body(
    mel_frames,
    frame_mask,
    token_ids,
    token_mask,
    embedding,
    conv_one,
    conv_two,
    enc_qkv,
    enc_out,
    enc_up,
    enc_down,
    cross_qkv,
    cross_out,
    dec_qkv,
    dec_out,
    dec_up,
    dec_down,
    norm_params,
    cotangent,
):
    dp_place = lax.axis_index("dp")
    frames = mel_frames.shape[0] // 2
    tokens = cotangent.shape[0]
    model_width = cotangent.shape[1]
    gathered = (
        lax.all_gather(conv_one, "dp", axis=2, tiled=True),
        lax.all_gather(conv_two, "dp", axis=1, tiled=True),
        lax.all_gather(enc_qkv, "dp", axis=1, tiled=True),
        lax.all_gather(enc_out, "dp", axis=1, tiled=True),
        lax.all_gather(enc_up, "dp", axis=0, tiled=True),
        lax.all_gather(enc_down, "dp", axis=1, tiled=True),
        lax.all_gather(cross_qkv, "dp", axis=1, tiled=True),
        lax.all_gather(cross_out, "dp", axis=1, tiled=True),
        lax.all_gather(dec_qkv, "dp", axis=1, tiled=True),
        lax.all_gather(dec_out, "dp", axis=1, tiled=True),
        lax.all_gather(dec_up, "dp", axis=0, tiled=True),
        lax.all_gather(dec_down, "dp", axis=1, tiled=True),
        lax.all_gather(norm_params, "dp", axis=2, tiled=True),
    )
    (
        full_conv_one,
        full_conv_two,
        full_enc_qkv,
        full_enc_out,
        full_enc_up,
        full_enc_down,
        full_cross_qkv,
        full_cross_out,
        full_dec_qkv,
        full_dec_out,
        full_dec_up,
        full_dec_down,
        full_norms,
    ) = gathered
    frame_row = lax.dynamic_index_in_dim(frame_mask, dp_place, 0, keepdims=False) > 0
    token_row = lax.dynamic_index_in_dim(token_mask, dp_place, 0, keepdims=False) > 0
    frame_allowed = frame_row[None, :]
    stem_sum = branch_sum(stem_piece(mel_frames, full_conv_one, full_conv_two))
    stream_zero = gelu_exact(stem_sum) + sinusoid(jnp.arange(frames, dtype=jnp.int32), model_width)
    enc_query, enc_keys, enc_values = project_three(stream_zero, full_norms[0], full_enc_qkv)
    enc_query_heads = split_heads(enc_query)
    enc_key_all = split_heads(enc_keys)
    enc_value_all = split_heads(enc_values)
    enc_mixed, enc_log_total = attend(enc_query_heads, enc_key_all, enc_value_all, frame_allowed)
    enc_mixed_flat = enc_mixed.reshape(frames, -1)
    enc_attn = branch_sum(matmul(enc_mixed_flat, full_enc_out))
    stream_one = stream_zero + enc_attn
    enc_mlp = branch_sum(feed_forward(stream_one, full_norms[1], full_enc_up, full_enc_down))
    stream_two = stream_one + enc_mlp
    cross_keys, cross_values = project_pair(
        stream_two, full_norms[2], full_cross_qkv[1], full_cross_qkv[2]
    )
    cross_key_all = split_heads(cross_keys)
    cross_value_all = split_heads(cross_values)
    flat_ids = token_ids.reshape(-1)
    vocab_rows = embedding.shape[0]
    local_ids = flat_ids - dp_place * vocab_rows
    owned_flags = (local_ids >= 0) & (local_ids < vocab_rows)
    safe_ids = jnp.clip(local_ids, 0, vocab_rows - 1)
    id_block = safe_ids
    flag_block = owned_flags
    picked = jnp.take(embedding, id_block, axis=0)
    embed_share = lax.psum_scatter(
        jnp.where(flag_block[:, None], picked, 0.0), "dp", scatter_dimension=0, tiled=True
    )
    embedded = lax.all_gather(embed_share, "mp", axis=1, tiled=True)
    text_zero = embedded + sinusoid(jnp.arange(tokens, dtype=jnp.int32), model_width)
    dec_query, dec_keys, dec_values = project_three(text_zero, full_norms[3], full_dec_qkv)
    positions = jnp.arange(tokens)
    self_allowed = (positions[None, :] <= positions[:, None]) & token_row[None, :]
    dec_query_heads = split_heads(dec_query)
    dec_key_all = split_heads(dec_keys)
    dec_value_all = split_heads(dec_values)
    dec_mixed, dec_log_total = attend(dec_query_heads, dec_key_all, dec_value_all, self_allowed)
    dec_mixed_flat = dec_mixed.reshape(tokens, -1)
    dec_attn = branch_sum(matmul(dec_mixed_flat, full_dec_out))
    text_one = text_zero + dec_attn
    cross_query = project_one(text_one, full_norms[4], full_cross_qkv[0])
    cross_query_heads = split_heads(cross_query)
    cross_mixed, cross_log_total = attend(
        cross_query_heads, cross_key_all, cross_value_all, frame_allowed
    )
    cross_mixed_flat = cross_mixed.reshape(tokens, -1)
    cross_attn = branch_sum(matmul(cross_mixed_flat, full_cross_out))
    text_two = text_one + cross_attn
    dec_mlp = branch_sum(feed_forward(text_two, full_norms[5], full_dec_up, full_dec_down))
    decoded = text_two + dec_mlp
    frame_weight = frame_row.astype(jnp.float32)
    token_weight = token_row.astype(jnp.float32)
    local_sums = jnp.stack(
        [
            masked_squares(stream_zero, frame_weight),
            masked_squares(enc_attn, frame_weight),
            masked_squares(enc_mlp, frame_weight),
            masked_squares(stream_two, frame_weight),
            masked_squares(text_zero, token_weight),
            masked_squares(dec_attn, token_weight),
            masked_squares(cross_attn, token_weight),
            masked_squares(dec_mlp, token_weight),
            masked_squares(decoded, token_weight),
        ]
    )
    square_sums = lax.psum(local_sums, "dp")
    frame_total = jnp.sum((frame_mask > 0).astype(jnp.float32))
    token_total = jnp.sum((token_mask > 0).astype(jnp.float32))
    counts = jnp.concatenate([jnp.full((4,), frame_total), jnp.full((5,), token_total)])
    rms_stats = jnp.sqrt(square_sums / (counts * model_width))
    grad_part, grad_norm_five, grad_dec_up, grad_dec_down = jax.vjp(
        feed_forward, text_two, full_norms[5], full_dec_up, full_dec_down
    )[1](cotangent)
    grad_summed, grad_norm_five = input_sum(grad_part, grad_norm_five)
    grad_text_two = cotangent + grad_summed
    grad_cross_out = matmul(cross_mixed_flat.T, grad_text_two)
    grad_cross_mixed = matmul(grad_text_two, full_cross_out.T)
    grad_cross_query, grad_cross_keys, grad_cross_values = attention_grads(
        cross_query_heads,
        cross_key_all,
        cross_value_all,
        frame_allowed,
        cross_mixed,
        cross_log_total,
        grad_cross_mixed,
    )
    grad_part, grad_norm_four, grad_cross_wq = jax.vjp(
        project_one, text_one, full_norms[4], full_cross_qkv[0]
    )[1](grad_cross_query)
    grad_summed, grad_norm_four = input_sum(grad_part, grad_norm_four)
    grad_text_one = grad_text_two + grad_summed
    grad_dec_out = matmul(dec_mixed_flat.T, grad_text_one)
    grad_dec_mixed = matmul(grad_text_one, full_dec_out.T)
    grad_dec_query, grad_dec_keys, grad_dec_values = attention_grads(
        dec_query_heads,
        dec_key_all,
        dec_value_all,
        self_allowed,
        dec_mixed,
        dec_log_total,
        grad_dec_mixed,
    )
    grad_part, grad_norm_three, grad_dec_qkv = jax.vjp(
        project_three, text_zero, full_norms[3], full_dec_qkv
    )[1]((grad_dec_query, grad_dec_keys, grad_dec_values))
    grad_summed, grad_norm_three = input_sum(grad_part, grad_norm_three)
    grad_text_zero = grad_text_one + grad_summed
    mp_place = lax.axis_index("mp")
    embed_width = embedding.shape[1]
    grad_embed_share = lax.dynamic_slice_in_dim(
        grad_text_zero, mp_place * embed_width, embed_width, 1
    )
    id_block = safe_ids
    flag_block = owned_flags
    grad_embedding = (
        jnp.zeros(embedding.shape, jnp.float32)
        .at[id_block]
        .add(
            jnp.where(
                flag_block[:, None], lax.all_gather(grad_embed_share, "dp", axis=0, tiled=True), 0.0
            )
        )
    )
    grad_part, grad_norm_two, grad_cross_wk, grad_cross_wv = jax.vjp(
        project_pair, stream_two, full_norms[2], full_cross_qkv[1], full_cross_qkv[2]
    )[1]((grad_cross_keys, grad_cross_values))
    grad_cross_qkv = jnp.stack([grad_cross_wq, grad_cross_wk, grad_cross_wv])
    grad_stream_two, grad_norm_two = input_sum(grad_part, grad_norm_two)
    grad_part, grad_norm_one, grad_enc_up, grad_enc_down = jax.vjp(
        feed_forward, stream_one, full_norms[1], full_enc_up, full_enc_down
    )[1](grad_stream_two)
    grad_summed, grad_norm_one = input_sum(grad_part, grad_norm_one)
    grad_stream_one = grad_stream_two + grad_summed
    grad_enc_out = matmul(enc_mixed_flat.T, grad_stream_one)
    grad_enc_mixed = matmul(grad_stream_one, full_enc_out.T)
    grad_enc_query, grad_enc_keys, grad_enc_values = attention_grads(
        enc_query_heads,
        enc_key_all,
        enc_value_all,
        frame_allowed,
        enc_mixed,
        enc_log_total,
        grad_enc_mixed,
    )
    grad_part, grad_norm_zero, grad_enc_qkv = jax.vjp(
        project_three, stream_zero, full_norms[0], full_enc_qkv
    )[1]((grad_enc_query, grad_enc_keys, grad_enc_values))
    grad_summed, grad_norm_zero = input_sum(grad_part, grad_norm_zero)
    grad_stream_zero = grad_stream_one + grad_summed
    grad_stem = jax.vjp(gelu_exact, stem_sum)[1](grad_stream_zero)[0]
    grad_mel_part, grad_conv_one, grad_conv_two = jax.vjp(
        stem_piece, mel_frames, full_conv_one, full_conv_two
    )[1](grad_stem)
    grad_mel = branch_sum(grad_mel_part)
    grad_norms = jnp.stack(
        [
            grad_norm_zero,
            grad_norm_one,
            grad_norm_two,
            grad_norm_three,
            grad_norm_four,
            grad_norm_five,
        ]
    )
    all_parts = tuple(
        (
            lax.psum_scatter(grad_conv_one, "dp", scatter_dimension=2, tiled=True),
            lax.psum_scatter(grad_conv_two, "dp", scatter_dimension=1, tiled=True),
            lax.psum_scatter(grad_enc_qkv, "dp", scatter_dimension=1, tiled=True),
            lax.psum_scatter(grad_enc_out, "dp", scatter_dimension=1, tiled=True),
            lax.psum_scatter(grad_enc_up, "dp", scatter_dimension=0, tiled=True),
            lax.psum_scatter(grad_enc_down, "dp", scatter_dimension=1, tiled=True),
            lax.psum_scatter(grad_cross_qkv, "dp", scatter_dimension=1, tiled=True),
            lax.psum_scatter(grad_cross_out, "dp", scatter_dimension=1, tiled=True),
            lax.psum_scatter(grad_dec_qkv, "dp", scatter_dimension=1, tiled=True),
            lax.psum_scatter(grad_dec_out, "dp", scatter_dimension=1, tiled=True),
            lax.psum_scatter(grad_dec_up, "dp", scatter_dimension=0, tiled=True),
            lax.psum_scatter(grad_dec_down, "dp", scatter_dimension=1, tiled=True),
            lax.psum_scatter(grad_norms, "dp", scatter_dimension=2, tiled=True),
        )
    )
    return (decoded, grad_mel, grad_embedding) + all_parts + (rms_stats,)


def solution(mesh):
    placed = (
        P("dp", None),
        P(),
        P(),
        P(),
        P("dp", "mp"),
        P(None, None, ("dp", "mp")),
        P(None, ("dp", "mp"), None),
        P(None, "dp", "mp"),
        P("mp", "dp"),
        P("dp", "mp"),
        P("mp", "dp"),
        P(None, "dp", "mp"),
        P("mp", "dp"),
        P(None, "dp", "mp"),
        P("mp", "dp"),
        P("dp", "mp"),
        P("mp", "dp"),
        P(None, None, "dp"),
        P("dp", None),
    )
    return jax.shard_map(
        body,
        mesh=mesh,
        in_specs=placed,
        out_specs=(
            P("dp", None),
            P("dp", None),
            P("dp", "mp"),
            P(None, None, ("dp", "mp")),
            P(None, ("dp", "mp"), None),
            P(None, "dp", "mp"),
            P("mp", "dp"),
            P("dp", "mp"),
            P("mp", "dp"),
            P(None, "dp", "mp"),
            P("mp", "dp"),
            P(None, "dp", "mp"),
            P("mp", "dp"),
            P("dp", "mp"),
            P("mp", "dp"),
            P(None, None, "dp"),
            P(),
        ),
        check_vma=False,
    )
```

profile of v0, /device:TPU:0, one launch (start us, length us, event | category | flops | bytes accessed | tf_op | source)
XLA Modules:
  0.0 2458.1 jit_solution(10924375323496480957)
XLA Ops:
  168.9 34.4 %all_gather.52 = f32[192,768]{0,1:T(8,128)} all-gather(f32[192,96]{0,1:T(8,128)S(1)} %copy.130), channel_id=1, replica_groups=mesh['dp'=8,'mp'=4] {'dp'}, dimensions={1}, use_global_device_ids=true | all-gather | bytes 663552 | tf_op jit(solution)/shard_map/all_gather | solution.py:144
  424.4 49.7 %all-gather.19.cloned.1.call-done = f32[768,768]{1,0:T(8,128)} async-done(((f32[96,768]{1,0:T(8,128)}), f32[768,768]{1,0:T(8,128)}) %all-gather.19.cloned.1.call-update) | async-done | bytes 2359312 | tf_op jit(solution)/shard_map/all_gather | solution.py:145
  492.0 34.7 %all-gather.21.cloned.1.call-done = f32[768,768]{0,1:T(8,128)} async-done(((f32[768,96]{0,1:T(8,128)}), f32[768,768]{0,1:T(8,128)}) %all-gather.21.cloned.1.call-update) | async-done | bytes 2359312 | tf_op jit(solution)/shard_map/all_gather | solution.py:146
  561.7 34.5 %all_gather.56 = f32[192,768]{0,1:T(8,128)S(1)} all-gather(f32[192,96]{0,1:T(8,128)S(1)} %copy.134), channel_id=1, replica_groups=mesh['dp'=8,'mp'=4] {'dp'}, dimensions={1}, use_global_device_ids=true | all-gather | bytes 663552 | tf_op jit(solution)/shard_map/all_gather | solution.py:148
  614.8 82.0 %all-reduce.67.cloned.1.call-done = (f32[384,768]{1,0:T(8,128)}, f32[1024,768]{1,0:T(8,128)}) async-done(((f32[384,768]{1,0:T(8,128)}, f32[1024,768]{1,0:T(8,128)}), (f32[384,768]{1,0:T(8,128)}, f32[1024,768]{1,0:T(8,128)})) %all-reduce.67.cloned.1.call-update) | async-done | bytes 4325392 | tf_op jit(solution)/shard_map/psum | solution.py:108
  755.6 34.5 %all-reduce.53.cloned.1.call-done = f32[384,768]{1,0:T(8,128)} async-done(((f32[384,768]{1,0:T(8,128)}), f32[384,768]{1,0:T(8,128)}) %all-reduce.53.cloned.1.call-update) | async-done | bytes 1179664 | tf_op jit(solution)/shard_map/psum | solution.py:108
  794.0 50.1 %all-gather.25.cloned.1.call-done = f32[768,768]{1,0:T(8,128)} async-done(((f32[96,768]{1,0:T(8,128)}), f32[768,768]{1,0:T(8,128)}) %all-gather.25.cloned.1.call-update) | async-done | bytes 2359312 | tf_op jit(solution)/shard_map/all_gather | solution.py:151
  858.0 36.2 %all-reduce.55.cloned.1.call-done = f32[384,768]{1,0:T(8,128)} async-done(((f32[384,768]{1,0:T(8,128)}), f32[384,768]{1,0:T(8,128)}) %all-reduce.55.cloned.1.call-update) | async-done | bytes 1179664 | tf_op jit(solution)/shard_map/psum | solution.py:112
  930.7 68.0 %all-reduce.57.cloned.1.call-done = f32[1024,768]{1,0:T(8,128)} async-done(((f32[1024,768]{1,0:T(8,128)}), f32[1024,768]{1,0:T(8,128)}) %all-reduce.57.cloned.1.call-update) | async-done | bytes 3145744 | tf_op jit(solution)/shard_map/psum | solution.py:112
  1041.5 54.6 %all-reduce.59.cloned.1.call-done = f32[1024,768]{1,0:T(8,128)} async-done(((f32[1024,768]{1,0:T(8,128)}), f32[1024,768]{1,0:T(8,128)}) %all-reduce.59.cloned.1.call-update) | async-done | bytes 3145744 | tf_op jit(solution)/shard_map/psum | solution.py:112
  1186.2 79.2 %all-reduce.65.cloned.1.call-done = (f32[1024,768]{1,0:T(8,128)}, f32[384,768]{1,0:T(8,128)}) async-done(((f32[1024,768]{1,0:T(8,128)}, f32[384,768]{1,0:T(8,128)}), (f32[1024,768]{1,0:T(8,128)}, f32[384,768]{1,0:T(8,128)})) %all-reduce.65.cloned.1.call-update) | async-done | bytes 4325392 | tf_op jit(solution)/shard_map/psum | solution.py:112
  1583.1 34.6 %reduce-scatter.44.cloned.1.call-done = f32[96,576]{1,0:T(8,128)} async-done(((f32[768,576]{1,0:T(8,128)}), f32[96,576]{1,0:T(8,128)}) %reduce-scatter.44.cloned.1.call-update) | async-done | bytes 221200
  1621.4 61.9 %reduce-scatter.42.cloned.1.call-done = f32[96,192]{1,0:T(8,128)} async-done(((f32[768,192]{1,0:T(8,128)}), f32[96,192]{1,0:T(8,128)}) %reduce-scatter.42.cloned.1.call-update) | async-done | bytes 73744
  1684.9 63.0 %reduce-scatter.52.cloned.1.call-done = f32[96,12]{1,0:T(8,128)} async-done(((f32[768,12]{1,0:T(8,128)}), f32[96,12]{1,0:T(8,128)}) %reduce-scatter.52.cloned.1.call-update) | async-done | bytes 4624
  1751.3 70.6 %all-reduce.61.cloned.1.call-done = f32[3,80,192]{1,0,2:T(4,128)} async-done(((f32[3,80,192]{1,0,2:T(4,128)}), f32[3,80,192]{1,0,2:T(4,128)}) %all-reduce.61.cloned.1.call-update) | async-done | bytes 184336
  1823.3 64.2 %reduce-scatter.50.cloned.1.call-done = f32[96,192]{1,0:T(8,128)} async-done(((f32[768,192]{1,0:T(8,128)}), f32[96,192]{1,0:T(8,128)}) %reduce-scatter.50.cloned.1.call-update) | async-done | bytes 73744
  1889.2 68.3 %reduce-scatter.40.cloned.1.call-done = f32[96,576]{1,0:T(8,128)} async-done(((f32[768,576]{1,0:T(8,128)}), f32[96,576]{1,0:T(8,128)}) %reduce-scatter.40.cloned.1.call-update) | async-done | bytes 221200
  1991.5 35.7 %reduce-scatter.48.cloned.1.call-done = f32[96,576]{1,0:T(8,128)} async-done(((f32[768,576]{1,0:T(8,128)}), f32[96,576]{1,0:T(8,128)}) %reduce-scatter.48.cloned.1.call-update) | async-done | bytes 221200
  2029.1 59.7 %all-gather.29.cloned.1.call-done = f32[3072,192]{1,0:T(8,128)} async-done(((f32[384,192]{1,0:T(8,128)}), f32[3072,192]{1,0:T(8,128)}) %all-gather.29.cloned.1.call-update) | async-done | bytes 2359312 | tf_op jit(solution)/shard_map/all_gather | solution.py:292
  2120.7 40.6 %reduce-scatter.38.cloned.1.call-done = f32[768,96]{0,1:T(8,128)} async-done(((f32[768,768]{0,1:T(8,128)}), f32[768,96]{0,1:T(8,128)}) %reduce-scatter.38.cloned.1.call-update) | async-done | bytes 294928 | tf_op jit(solution)/shard_map/reduce_scatter | solution.py:350
  2161.3 72.9 %reduce-scatter.36.cloned.1.call-done = f32[96,768]{1,0:T(8,128)} async-done(((f32[768,768]{1,0:T(8,128)}), f32[96,768]{1,0:T(8,128)}) %reduce-scatter.36.cloned.1.call-update) | async-done | bytes 294928 | tf_op jit(solution)/shard_map/reduce_scatter | solution.py:349
  2234.2 73.1 %reduce-scatter.34.cloned.1.call-done = f32[768,96]{0,1:T(8,128)} async-done(((f32[768,768]{0,1:T(8,128)}), f32[768,96]{0,1:T(8,128)}) %reduce-scatter.34.cloned.1.call-update) | async-done | bytes 294928 | tf_op jit(solution)/shard_map/reduce_scatter | solution.py:344
  2307.3 73.1 %reduce-scatter.32.cloned.1.call-done = f32[96,768]{1,0:T(8,128)} async-done(((f32[768,768]{1,0:T(8,128)}), f32[96,768]{1,0:T(8,128)}) %reduce-scatter.32.cloned.1.call-update) | async-done | bytes 294928 | tf_op jit(solution)/shard_map/reduce_scatter | solution.py:343
  2380.4 69.6 %reduce-scatter.30.cloned.1.call-done = f32[3,24,768]{2,1,0:T(8,128)} async-done(((f32[3,192,768]{2,1,0:T(8,128)}), f32[3,24,768]{2,1,0:T(8,128)}) %reduce-scatter.30.cloned.1.call-update) | async-done | bytes 221200 | tf_op jit(solution)/shard_map/reduce_scatter | solution.py:340
  (780 shorter events, 1093.3 us)
Async XLA Ops:
  7.9 270.1 %all-gather.17.cloned.1.call-start = ((), (), s32[]{:S(2)}) async-start(), calls=%async_computation.18 | async-start | bytes 2654208 | tf_op jit(solution)/shard_map/all_gather | solution.py:143
  8.7 274.3 %all-reduce.49.cloned.1.call-start = ((), (), s32[]{:S(2)}) async-start(), calls=%async_computation.17 | async-start | bytes 6291456 | tf_op jit(solution)/shard_map/psum | solution.py:108
  145.0 197.1 %reduce-scatter.28.cloned.1.call-start = ((), (), s32[]{:S(2)}) async-start(), calls=%async_computation.13 | async-start | bytes 3538944 | tf_op jit(solution)/shard_map/reduce_scatter | solution.py:198
  167.7 215.0 %all-gather.13.cloned.1.call-start = ((), (), s32[]{:S(2)}) async-start(), calls=%async_computation.15 | async-start | bytes 2654208 | tf_op jit(solution)/shard_map/all_gather | solution.py:149
  168.3 251.6 %all-reduce.51.cloned.1.call-start = ((), (), s32[]{:S(2)}) async-start(), calls=%async_computation.19 | async-start | bytes 6291456 | tf_op jit(solution)/shard_map/psum | solution.py:108
  342.0 202.8 %all-gather.11.cloned.1.call-start = ((), (), s32[]{:S(2)}) async-start(), calls=%async_computation.14 | async-start | bytes 1474560 | tf_op jit(solution)/shard_map/all_gather | solution.py:201
  343.9 262.5 %all-gather.23.cloned.1.call-start = ((), (), s32[]{:S(2)}) async-start(), calls=%async_computation.22 | async-start | bytes 2654208 | tf_op jit(solution)/shard_map/all_gather | solution.py:147
  344.5 352.3 %all-reduce.67.cloned.1.call-start = ((), (), s32[]{:S(2)}) async-start(), calls=%async_computation.45 | async-start | bytes 8650752 | tf_op jit(solution)/shard_map/psum | solution.py:108
  561.4 228.8 %all-reduce.53.cloned.1.call-start = ((), (), s32[]{:S(2)}) async-start(), calls=%async_computation.23 | async-start | bytes 2359296 | tf_op jit(solution)/shard_map/psum | solution.py:108
  1027.5 237.9 %all-reduce.65.cloned.1.call-start = ((), (), s32[]{:S(2)}) async-start(), calls=%async_computation.44 | async-start | bytes 8650752 | tf_op jit(solution)/shard_map/psum | solution.py:112
  1177.5 344.1 %all-reduce.63.cloned.1.call-start = ((), (), s32[]{:S(2)}) async-start(), calls=%async_computation.43 | async-start | bytes 6029312 | tf_op jit(solution)/shard_map/psum | solution.py:108
  1418.9 198.8 %reduce-scatter.44.cloned.1.call-start = ((), (), s32[]{:S(2)}) async-start(), calls=%async_computation.37 | async-start | bytes 2211840
  1440.9 242.4 %reduce-scatter.42.cloned.1.call-start = ((), (), s32[]{:S(2)}) async-start(), calls=%async_computation.36 | async-start | bytes 884736
  1449.4 298.4 %reduce-scatter.52.cloned.1.call-start = ((), (), s32[]{:S(2)}) async-start(), calls=%async_computation.41 | async-start | bytes 442368
  1474.4 347.5 %all-reduce.61.cloned.1.call-start = ((), (), s32[]{:S(2)}) async-start(), calls=%async_computation.42 | async-start | bytes 786432
  1478.0 409.6 %reduce-scatter.50.cloned.1.call-start = ((), (), s32[]{:S(2)}) async-start(), calls=%async_computation.40 | async-start | bytes 884736
  1482.4 475.0 %reduce-scatter.40.cloned.1.call-start = ((), (), s32[]{:S(2)}) async-start(), calls=%async_computation.35 | async-start | bytes 2211840
  1504.1 523.1 %reduce-scatter.48.cloned.1.call-start = ((), (), s32[]{:S(2)}) async-start(), calls=%async_computation.39 | async-start | bytes 2211840
  1521.6 567.3 %all-gather.29.cloned.1.call-start = ((), (), s32[]{:S(2)}) async-start(), calls=%async_computation.29 | async-start | bytes 3538944 | tf_op jit(solution)/shard_map/all_gather | solution.py:292
  1523.9 637.3 %reduce-scatter.38.cloned.1.call-start = ((), (), s32[]{:S(2)}) async-start(), calls=%async_computation.34 | async-start | bytes 2654208 | tf_op jit(solution)/shard_map/reduce_scatter | solution.py:350
  1531.5 702.8 %reduce-scatter.36.cloned.1.call-start = ((), (), s32[]{:S(2)}) async-start(), calls=%async_computation.33 | async-start | bytes 2654208 | tf_op jit(solution)/shard_map/reduce_scatter | solution.py:349
  1540.4 766.9 %reduce-scatter.34.cloned.1.call-start = ((), (), s32[]{:S(2)}) async-start(), calls=%async_computation.32 | async-start | bytes 2654208 | tf_op jit(solution)/shard_map/reduce_scatter | solution.py:344
  1552.6 827.8 %reduce-scatter.32.cloned.1.call-start = ((), (), s32[]{:S(2)}) async-start(), calls=%async_computation.31 | async-start | bytes 2654208 | tf_op jit(solution)/shard_map/reduce_scatter | solution.py:343
  1567.4 882.6 %reduce-scatter.30.cloned.1.call-start = ((), (), s32[]{:S(2)}) async-start(), calls=%async_computation.30 | async-start | bytes 1990656 | tf_op jit(solution)/shard_map/reduce_scatter | solution.py:340
  (230 other events, 10995.0 us)
Sparse Core Ops, SparseCore 0:
  145.1 69.0 all-reduce.48
  218.2 75.4 reduce-scatter.27
  295.7 55.1 all-gather.12
  353.1 66.8 all-reduce.50
  546.8 59.5 all-gather.22
  609.5 87.3 all-reduce.66
  930.1 68.5 all-reduce.56
  1027.6 68.5 all-reduce.58
  1177.6 87.7 all-reduce.64
  1414.4 66.8 all-reduce.62
  1484.4 63.3 reduce-scatter.45
  1551.3 66.4 reduce-scatter.43
  1621.0 62.1 reduce-scatter.41
  1686.5 61.2 reduce-scatter.51
  1751.1 70.7 all-reduce.60
  1825.2 62.2 reduce-scatter.49
  1890.9 66.5 reduce-scatter.39
  1960.8 66.4 reduce-scatter.47
  2030.0 58.8 all-gather.28
  2092.9 68.3 reduce-scatter.37
  2165.2 68.9 reduce-scatter.35
  2238.3 68.9 reduce-scatter.33
  2311.4 68.9 reduce-scatter.31
  2384.3 65.6 reduce-scatter.29
  (9 shorter events, 393.9 us)
where the time goes:
time: 2470 us; the launch traced here: 2460 us
  waiting for transfers between devices  1340 us (54%)
  matrix products  430 us (17%)
  local copies, waits for them, and re-layouts  334 us (14%)
  blocking collectives  200 us (8%)
  other arithmetic  126 us (5%)
    unnamed x41, waiting for transfers between devices  404 us
    dot_general x63, matrix products, matmul(): jnp.dot(left, right, precision=HIGH, preferred_element_type=jnp.float32)  296 us
    psum x4, waiting for transfers between devices, input_sum(): return lax.psum((grad_rows, grad_norm), 'mp')  238 us
    psum x5, waiting for transfers between devices, branch_sum(): return lax.psum(tensor, 'mp')  144 us
    unnamed x478, local copies, waits for them, and re-layouts  111 us
    reduce_scatter x1, waiting for transfers between devices, body(): lax.psum_scatter(grad_enc_down, 'dp', scatter_dimension=1, tiled=True)  73.1 us
    reduce_scatter x1, waiting for transfers between devices, body(): lax.psum_scatter(grad_enc_up, 'dp', scatter_dimension=0, tiled=True)  73.1 us
    reduce_scatter x1, waiting for transfers between devices, body(): lax.psum_scatter(grad_dec_up, 'dp', scatter_dimension=0, tiled=True)  72.9 us
  transfers between devices with their start and end apart: 33, of which 26 were waited for; matrix products, arithmetic and copies ran while one was open for 23% of the time, Pallas kernels for 0%

commit v1 on v0

--- a/solution.py
+++ b/solution.py
@@ -8,6 +8,11 @@
 HIGH = lax.Precision.HIGHEST
 NEG = -1e30
 EPS = 1e-05
+
+
+def add_all(array, mesh_axis):
+    pieces = lax.all_gather(array, mesh_axis)
+    return jnp.sum(pieces, axis=0)
 
 
 def matmul(left, right):
@@ -105,7 +110,7 @@
 
 
 def branch_sum(tensor):
-    return lax.psum(tensor, "mp")
+    return add_all(tensor, "mp")
 
 
 def input_sum(grad_rows, grad_norm):

time: 2470 us -> 2430 us (0.984)
  waiting for transfers between devices: 1340 us -> 1270 us
  other arithmetic: 126 us -> 160 us
    all_gather x0 -> x7, waiting for transfers between devices: none -> 221 us  [add_all(): pieces = lax.all_gather(array, mesh_axis)]
    psum x5 -> x0, waiting for transfers between devices: 144 us -> none  [branch_sum(): return lax.psum(tensor, 'mp')]
    unnamed x41 -> x43, waiting for transfers between devices: 404 us -> 280 us
    reduce_sum x0 -> x7, other arithmetic: none -> 33.9 us  [add_all(): return jnp.sum(pieces, axis=0)]
    reduce_scatter x1, waiting for transfers between devices: 40.6 us -> 73.1 us  [body(): lax.psum_scatter(grad_dec_down, 'dp', scatter_dimension=1, tiled=True)]
    reduce_scatter x1, waiting for transfers between devices: 72.9 us -> 40.6 us  [body(): lax.psum_scatter(grad_dec_up, 'dp', scatter_dimension=0, tiled=True)]
    psum x4, waiting for transfers between devices: 238 us -> 210 us  [input_sum(): return lax.psum((grad_rows, grad_norm), 'mp')]
    all_gather x1, waiting for transfers between devices: 18.8 us -> 43.9 us  [body(): lax.all_gather(dec_down, 'dp', axis=1, tiled=True)]
  transfers between devices with their start and end apart: 33 -> 35, of which waited for: 26 -> 26; matrix products, arithmetic and copies ran while one was open for 23% -> 28% of each run, Pallas kernels for 0% -> 0%
where the time goes in v1:
time: 2430 us
  waiting for transfers between devices  1270 us (52%)
  matrix products  443 us (18%)
  local copies, waits for them, and re-layouts  325 us (13%)
  blocking collectives  204 us (8%)
  other arithmetic  160 us (7%)
    dot_general x63, matrix products, matmul(): jnp.dot(left, right, precision=HIGH, preferred_element_type=jnp.float32)  309 us
    unnamed x43, waiting for transfers between devices  280 us
    all_gather x7, waiting for transfers between devices, add_all(): pieces = lax.all_gather(array, mesh_axis)  221 us
    psum x4, waiting for transfers between devices, input_sum(): return lax.psum((grad_rows, grad_norm), 'mp')  210 us
    unnamed x463, local copies, waits for them, and re-layouts  106 us
    reduce_scatter x1, waiting for transfers between devices, body(): lax.psum_scatter(grad_dec_down, 'dp', scatter_dimension=1, tiled=True)  73.1 us
    reduce_scatter x1, waiting for transfers between devices, body(): lax.psum_scatter(grad_enc_down, 'dp', scatter_dimension=1, tiled=True)  72.9 us
    reduce_scatter x1, waiting for transfers between devices, body(): lax.psum_scatter(grad_enc_up, 'dp', scatter_dimension=0, tiled=True)  72.8 us
  transfers between devices with their start and end apart: 35, of which 26 were waited for; matrix products, arithmetic and copies ran while one was open for 28% of the time, Pallas kernels for 0%

profile of v1, /device:TPU:0, one launch (start us, length us, event | category | flops | bytes accessed | tf_op | source)
XLA Modules:
  0.0 2426.0 jit_solution(14492148486295312881)
XLA Ops:
  33.5 33.6 %all_gather.93 = f32[3,80,192]{1,2,0:T(8,128)S(1)} all-gather(f32[3,80,24]{1,2,0:T(8,128)S(1)} %copy-done.159), channel_id=1, replica_groups=mesh['dp'=8,'mp'=4] {'dp'}, dimensions={2}, use_global_device_ids=true | all-gather | bytes 207360 | tf_op jit(solution)/shard_map/all_gather | solution.py:146
  170.6 33.9 %all_gather.88 = f32[6,2,768]{0,1,2:T(2,128)S(1)} all-gather(f32[6,2,96]{0,1,2:T(2,128)S(1)} %copy.120), channel_id=1, replica_groups=mesh['dp'=8,'mp'=4] {'dp'}, dimensions={2}, use_global_device_ids=true | all-gather | bytes 41472 | tf_op jit(solution)/shard_map/all_gather | solution.py:158
  204.5 33.8 %all_gather.98 = f32[192,768]{0,1:T(8,128)} all-gather(f32[192,96]{0,1:T(8,128)S(1)} %copy.130), channel_id=1, replica_groups=mesh['dp'=8,'mp'=4] {'dp'}, dimensions={1}, use_global_device_ids=true | all-gather | bytes 663552 | tf_op jit(solution)/shard_map/all_gather | solution.py:149
  448.5 41.0 %all-gather.33.cloned.1.call-done = f32[768,768]{1,0:T(8,128)} async-done(((f32[96,768]{1,0:T(8,128)}), f32[768,768]{1,0:T(8,128)}) %all-gather.33.cloned.1.call-update) | async-done | bytes 2359312 | tf_op jit(solution)/shard_map/all_gather | solution.py:150
  507.8 34.2 %all-gather.35.cloned.1.call-done = f32[768,768]{0,1:T(8,128)} async-done(((f32[768,96]{0,1:T(8,128)}), f32[768,768]{0,1:T(8,128)}) %all-gather.35.cloned.1.call-update) | async-done | bytes 2359312 | tf_op jit(solution)/shard_map/all_gather | solution.py:151
  554.8 36.2 %all_gather.106 = f32[192,768]{0,1:T(8,128)} all-gather(f32[192,96]{0,1:T(8,128)S(1)} %copy.134), channel_id=1, replica_groups=mesh['dp'=8,'mp'=4] {'dp'}, dimensions={1}, use_global_device_ids=true | all-gather | bytes 663552 | tf_op jit(solution)/shard_map/all_gather | solution.py:153
  605.7 34.4 %all-gather.45.cloned.1.call-done = f32[1536,768]{1,0:T(8,128)} async-done(((f32[384,768]{1,0:T(8,128)}), f32[1536,768]{1,0:T(8,128)}) %all-gather.45.cloned.1.call-update) | async-done | bytes 4718608 | tf_op jit(solution)/shard_map/all_gather | solution.py:14
  646.3 77.4 %all-gather.51.cloned.1.call-done = f32[4096,768]{1,0:T(8,128)} async-done(((f32[1024,768]{1,0:T(8,128)}), f32[4096,768]{1,0:T(8,128)}) %all-gather.51.cloned.1.call-update) | async-done | bytes 12582928 | tf_op jit(solution)/shard_map/all_gather | solution.py:14
  763.8 36.4 %all-gather.53.cloned.1.call-done = f32[1536,768]{1,0:T(8,128)} async-done(((f32[384,768]{1,0:T(8,128)}), f32[1536,768]{1,0:T(8,128)}) %all-gather.53.cloned.1.call-update) | async-done | bytes 4718608 | tf_op jit(solution)/shard_map/all_gather | solution.py:14
  808.0 46.1 %all-gather.39.cloned.1.call-done = f32[768,768]{1,0:T(8,128)} async-done(((f32[96,768]{1,0:T(8,128)}), f32[768,768]{1,0:T(8,128)}) %all-gather.39.cloned.1.call-update) | async-done | bytes 2359312 | tf_op jit(solution)/shard_map/all_gather | solution.py:156
  862.6 43.9 %all-gather.41.cloned.1.call-done = f32[768,768]{0,1:T(8,128)} async-done(((f32[768,96]{0,1:T(8,128)}), f32[768,768]{0,1:T(8,128)}) %all-gather.41.cloned.1.call-update) | async-done | bytes 2359312 | tf_op jit(solution)/shard_map/all_gather | solution.py:157
  959.8 36.8 %all-reduce.43.cloned.1.call-done = f32[384,768]{1,0:T(8,128)} async-done(((f32[384,768]{1,0:T(8,128)}), f32[384,768]{1,0:T(8,128)}) %all-reduce.43.cloned.1.call-update) | async-done | bytes 1179664 | tf_op jit(solution)/shard_map/psum | solution.py:117
  1060.6 55.5 %all-reduce.45.cloned.1.call-done = f32[1024,768]{1,0:T(8,128)} async-done(((f32[1024,768]{1,0:T(8,128)}), f32[1024,768]{1,0:T(8,128)}) %all-reduce.45.cloned.1.call-update) | async-done | bytes 3145744 | tf_op jit(solution)/shard_map/psum | solution.py:117
  1146.9 85.9 %all-reduce.51.cloned.1.call-done = (f32[1024,768]{1,0:T(8,128)}, f32[384,768]{1,0:T(8,128)}) async-done(((f32[1024,768]{1,0:T(8,128)}, f32[384,768]{1,0:T(8,128)}), (f32[1024,768]{1,0:T(8,128)}, f32[384,768]{1,0:T(8,128)})) %all-reduce.51.cloned.1.call-update) | async-done | bytes 4325392 | tf_op jit(solution)/shard_map/psum | solution.py:117
  1690.5 64.0 %reduce-scatter.50.cloned.1.call-done = f32[96,192]{1,0:T(8,128)} async-done(((f32[768,192]{1,0:T(8,128)}), f32[96,192]{1,0:T(8,128)}) %reduce-scatter.50.cloned.1.call-update) | async-done | bytes 73744
  1756.1 72.4 %all-reduce.47.cloned.1.call-done = f32[3,80,192]{1,0,2:T(4,128)} async-done(((f32[3,80,192]{1,0,2:T(4,128)}), f32[3,80,192]{1,0,2:T(4,128)}) %all-reduce.47.cloned.1.call-update) | async-done | bytes 184336
  1830.0 68.5 %reduce-scatter.48.cloned.1.call-done = f32[96,576]{1,0:T(8,128)} async-done(((f32[768,576]{1,0:T(8,128)}), f32[96,576]{1,0:T(8,128)}) %reduce-scatter.48.cloned.1.call-update) | async-done | bytes 221200
  1900.4 68.3 %reduce-scatter.40.cloned.1.call-done = f32[96,576]{1,0:T(8,128)} async-done(((f32[768,576]{1,0:T(8,128)}), f32[96,576]{1,0:T(8,128)}) %reduce-scatter.40.cloned.1.call-update) | async-done | bytes 221200
  2001.3 56.6 %all-gather.43.cloned.1.call-done = f32[3072,192]{1,0:T(8,128)} async-done(((f32[384,192]{1,0:T(8,128)}), f32[3072,192]{1,0:T(8,128)}) %all-gather.43.cloned.1.call-update) | async-done | bytes 2359312 | tf_op jit(solution)/shard_map/all_gather | solution.py:297
  2089.7 40.6 %reduce-scatter.36.cloned.1.call-done = f32[96,768]{1,0:T(8,128)} async-done(((f32[768,768]{1,0:T(8,128)}), f32[96,768]{1,0:T(8,128)}) %reduce-scatter.36.cloned.1.call-update) | async-done | bytes 294928 | tf_op jit(solution)/shard_map/reduce_scatter | solution.py:354
  2130.3 73.1 %reduce-scatter.38.cloned.1.call-done = f32[768,96]{0,1:T(8,128)} async-done(((f32[768,768]{0,1:T(8,128)}), f32[768,96]{0,1:T(8,128)}) %reduce-scatter.38.cloned.1.call-update) | async-done | bytes 294928 | tf_op jit(solution)/shard_map/reduce_scatter | solution.py:355
  2203.4 72.9 %reduce-scatter.34.cloned.1.call-done = f32[768,96]{0,1:T(8,128)} async-done(((f32[768,768]{0,1:T(8,128)}), f32[768,96]{0,1:T(8,128)}) %reduce-scatter.34.cloned.1.call-update) | async-done | bytes 294928 | tf_op jit(solution)/shard_map/reduce_scatter | solution.py:349
  2276.4 72.8 %reduce-scatter.32.cloned.1.call-done = f32[96,768]{1,0:T(8,128)} async-done(((f32[768,768]{1,0:T(8,128)}), f32[96,768]{1,0:T(8,128)}) %reduce-scatter.32.cloned.1.call-update) | async-done | bytes 294928 | tf_op jit(solution)/shard_map/reduce_scatter | solution.py:348
  2349.2 70.1 %reduce-scatter.30.cloned.1.call-done = f32[3,24,768]{2,1,0:T(8,128)} async-done(((f32[3,192,768]{2,1,0:T(8,128)}), f32[3,24,768]{2,1,0:T(8,128)}) %reduce-scatter.30.cloned.1.call-update) | async-done | bytes 221200 | tf_op jit(solution)/shard_map/reduce_scatter | solution.py:345
  (777 shorter events, 1119.1 us)
Async XLA Ops:
  7.9 271.2 %all-gather.31.cloned.1.call-start = ((), (), s32[]{:S(2)}) async-start(), calls=%async_computation.17 | async-start | bytes 2654208 | tf_op jit(solution)/shard_map/all_gather | solution.py:148
  8.7 275.4 %reduce-scatter.28.cloned.1.call-start = ((), (), s32[]{:S(2)}) async-start(), calls=%async_computation.13 | async-start | bytes 3538944 | tf_op jit(solution)/shard_map/reduce_scatter | solution.py:203
  32.8 253.3 %all-gather.47.cloned.1.call-start = ((), (), s32[]{:S(2)}) async-start(), calls=%async_computation.32 | async-start | bytes 15728640 | tf_op jit(solution)/shard_map/all_gather | solution.py:14
  169.4 224.5 %all-gather.25.cloned.1.call-start = ((), (), s32[]{:S(2)}) async-start(), calls=%async_computation.14 | async-start | bytes 1474560 | tf_op jit(solution)/shard_map/all_gather | solution.py:206
  351.1 249.7 %all-gather.37.cloned.1.call-start = ((), (), s32[]{:S(2)}) async-start(), calls=%async_computation.20 | async-start | bytes 2654208 | tf_op jit(solution)/shard_map/all_gather | solution.py:152
  351.6 288.5 %all-gather.45.cloned.1.call-start = ((), (), s32[]{:S(2)}) async-start(), calls=%async_computation.31 | async-start | bytes 5898240 | tf_op jit(solution)/shard_map/all_gather | solution.py:14
  409.9 313.8 %all-gather.51.cloned.1.call-start = ((), (), s32[]{:S(2)}) async-start(), calls=%async_computation.34 | async-start | bytes 15728640 | tf_op jit(solution)/shard_map/all_gather | solution.py:14
  553.8 246.4 %all-gather.53.cloned.1.call-start = ((), (), s32[]{:S(2)}) async-start(), calls=%async_computation.35 | async-start | bytes 5898240 | tf_op jit(solution)/shard_map/all_gather | solution.py:14
  1144.8 277.2 %all-reduce.49.cloned.1.call-start = ((), (), s32[]{:S(2)}) async-start(), calls=%async_computation.46 | async-start | bytes 8650752 | tf_op jit(solution)/shard_map/psum | solution.py:117
  1333.3 320.0 %reduce-scatter.46.cloned.1.call-start = ((), (), s32[]{:S(2)}) async-start(), calls=%async_computation.41 | async-start | bytes 884736
  1337.3 317.6 %reduce-scatter.44.cloned.1.call-start = ((), (), s32[]{:S(2)}) async-start(), calls=%async_computation.40 | async-start | bytes 2211840
  1355.7 330.2 %reduce-scatter.52.cloned.1.call-start = ((), (), s32[]{:S(2)}) async-start(), calls=%async_computation.44 | async-start | bytes 442368
  1374.5 314.4 %reduce-scatter.42.cloned.1.call-start = ((), (), s32[]{:S(2)}) async-start(), calls=%async_computation.39 | async-start | bytes 884736
  1382.8 371.7 %reduce-scatter.50.cloned.1.call-start = ((), (), s32[]{:S(2)}) async-start(), calls=%async_computation.43 | async-start | bytes 884736
  1390.3 438.2 %all-reduce.47.cloned.1.call-start = ((), (), s32[]{:S(2)}) async-start(), calls=%async_computation.45 | async-start | bytes 786432
  1554.5 344.1 %reduce-scatter.48.cloned.1.call-start = ((), (), s32[]{:S(2)}) async-start(), calls=%async_computation.42 | async-start | bytes 2211840
  1567.6 401.1 %reduce-scatter.40.cloned.1.call-start = ((), (), s32[]{:S(2)}) async-start(), calls=%async_computation.38 | async-start | bytes 2211840
  1589.5 405.7 %all-gather.57.cloned.1.call-start = ((), (), s32[]{:S(2)}) async-start(), calls=%async_computation.37 | async-start | bytes 3276800 | tf_op jit(solution)/shard_map/all_gather | solution.py:14
  1595.7 462.2 %all-gather.43.cloned.1.call-start = ((), (), s32[]{:S(2)}) async-start(), calls=%async_computation.25 | async-start | bytes 3538944 | tf_op jit(solution)/shard_map/all_gather | solution.py:297
  1598.0 532.3 %reduce-scatter.36.cloned.1.call-start = ((), (), s32[]{:S(2)}) async-start(), calls=%async_computation.29 | async-start | bytes 2654208 | tf_op jit(solution)/shard_map/reduce_scatter | solution.py:354
  1606.4 597.0 %reduce-scatter.38.cloned.1.call-start = ((), (), s32[]{:S(2)}) async-start(), calls=%async_computation.30 | async-start | bytes 2654208 | tf_op jit(solution)/shard_map/reduce_scatter | solution.py:355
  1614.1 662.3 %reduce-scatter.34.cloned.1.call-start = ((), (), s32[]{:S(2)}) async-start(), calls=%async_computation.28 | async-start | bytes 2654208 | tf_op jit(solution)/shard_map/reduce_scatter | solution.py:349
  1626.4 722.8 %reduce-scatter.32.cloned.1.call-start = ((), (), s32[]{:S(2)}) async-start(), calls=%async_computation.27 | async-start | bytes 2654208 | tf_op jit(solution)/shard_map/reduce_scatter | solution.py:348
  1641.1 778.1 %reduce-scatter.30.cloned.1.call-start = ((), (), s32[]{:S(2)}) async-start(), calls=%async_computation.26 | async-start | bytes 1990656 | tf_op jit(solution)/shard_map/reduce_scatter | solution.py:345
  (225 other events, 7347.3 us)
Sparse Core Ops, SparseCore 0:
  10.2 51.9 all-gather.28
  118.8 77.1 reduce-scatter.27
  197.4 81.8 all-gather.46
  281.3 51.8 all-gather.26
  353.3 82.0 all-gather.48
  544.1 56.6 all-gather.36
  641.6 82.0 all-gather.50
  1047.5 68.5 all-reduce.44
  1145.0 87.7 all-reduce.50
  1333.4 88.5 all-reduce.48
  1425.3 63.3 reduce-scatter.45
  1492.2 66.6 reduce-scatter.43
  1562.1 61.2 reduce-scatter.51
  1626.5 62.3 reduce-scatter.41
  1692.2 62.2 reduce-scatter.49
  1757.7 70.8 all-reduce.46
  1831.9 66.5 reduce-scatter.47
  1902.0 66.6 reduce-scatter.39
  1997.8 59.9 all-gather.42
  2062.0 68.3 reduce-scatter.35
  2134.4 68.9 reduce-scatter.37
  2207.3 68.9 reduce-scatter.33
  2280.4 68.7 reduce-scatter.31
  2353.2 65.9 reduce-scatter.29
  (11 shorter events, 442.5 us)
